TPU v7x, 32 devices: a whole 2x2x4 slice. The times are simulated.
32 devices in a mesh: fsdp: 8 (over y, x, core), seq: 4 (over z).
Axes of the slice: x: 2, y: 2, z: 4, core: 2. Of those that a mesh axis runs over, the one named last changes fastest.
Arguments:
- inputs: bfloat16 [3, 8, 1024, 1024], P(None, 'fsdp', 'seq'), may hold values from -6 to 6
- segment_ids: int32 [3, 8, 1024], P(None, 'fsdp'), may hold values from 0 to 3, never falling along the last dimension, each value on 1 to 512 neighbouring positions
- buckets: int32 [1024], replicated, may hold values from 0 to 31, as said below
- ln1_gain: bfloat16 [1024], P('fsdp'), may hold values from 0.5 to 1.5
- ln1_bias: bfloat16 [1024], P('fsdp'), may hold values from -3 to 3
- w_query: bfloat16 [1024, 1024], P('fsdp'), may hold values from -0.1875 to 0.1875
- w_key: bfloat16 [1024, 1024], P('fsdp'), may hold values from -0.1875 to 0.1875
- w_value: bfloat16 [1024, 1024], P('fsdp'), may hold values from -0.1875 to 0.1875
- w_out: bfloat16 [1024, 1024], P('fsdp'), may hold values from -0.75 to 0.75
- rel_bias: bfloat16 [32, 16], P('fsdp'), may hold values from -4 to 4
- second_norm_gain: bfloat16 [1024], P('fsdp'), may hold values from 0.5 to 1.5
- ln2_bias: bfloat16 [1024], P('fsdp'), may hold values from -3 to 3
- w_up: bfloat16 [1024, 4096], P('fsdp'), may hold values from -0.1875 to 0.1875
- b_up: bfloat16 [4096], P('fsdp'), may hold values from -3 to 3
- w_down: bfloat16 [4096, 1024], P('fsdp'), may hold values from -0.09375 to 0.09375
- b_down: bfloat16 [1024], P('fsdp'), may hold values from -3 to 3
- cotangent: bfloat16 [3, 8, 1024, 1024], P(None, 'fsdp', 'seq'), may hold values from -6 to 6
Outputs:
- outputs: bfloat16 [3, 8, 1024, 1024], P(None, 'fsdp', 'seq')
- input_grad: bfloat16 [3, 8, 1024, 1024], P(None, 'fsdp', 'seq')
- grad_ln1_gain: float32 [1024], P('fsdp')
- grad_ln1_bias: float32 [1024], P('fsdp')
- grad_w_query: float32 [1024, 1024], P('fsdp')
- grad_w_key: float32 [1024, 1024], P('fsdp')
- grad_w_value: float32 [1024, 1024], P('fsdp')
- grad_w_out: float32 [1024, 1024], P('fsdp')
- grad_rel_bias: float32 [32, 16], P('fsdp')
- grad_ln2_gain: float32 [1024], P('fsdp')
- grad_ln2_bias: float32 [1024], P('fsdp')
- grad_w_up: float32 [1024, 4096], P('fsdp')
- grad_b_up: float32 [4096], P('fsdp')
- grad_w_down: float32 [4096, 1024], P('fsdp')
- grad_b_down: float32 [1024], P('fsdp')
Inputs may be any that keep to these rules, and one draw needn't show every extreme that they name: `segment_ids`: along a row the clip number never falls; each clip of a row has 1 to 512 tokens, and some clip has exactly 512. `buckets`: the bucket never falls as the distance grows; it is 0 at distance 0 and 31 at distance 1024 - 1.
All inputs are finite; a program needn't handle non-finite values.
Results may differ from a plain program's by a relative error of at most 0.025.
Values may be sent and summed in bfloat16 or wider, within the bound.
No kernel may reach another device: no remote copies, remote signals or barrier semaphores. Data moves between devices by JAX's collectives and lax.ppermute only.
A program may use at most 448 MiB of HBM per device.

v0:
```python
import jax
import jax.numpy as jnp
from jax import lax
from jax.sharding import PartitionSpec as P

epsilon = 1e-05
masked_out = -1e30
EXACT_PRECISION = lax.Precision.HIGHEST


def layer_norm(field, norm_gain, norm_shift):
    centre = field - jnp.mean(field, axis=-1, keepdims=True)
    spread = jnp.mean(centre * centre, axis=-1, keepdims=True)
    return centre * lax.rsqrt(spread + epsilon) * norm_gain + norm_shift


def gelu_exact(field):
    return jax.nn.gelu(field, approximate=False)


def token_dot(left, right):
    return lax.dot_general(
        left, right, (((0,), (0,)), ((), ())), preferred_element_type=jnp.float32
    )


def back_dot(left, right):
    return lax.dot_general(
        left, right, (((1,), (1,)), ((), ())), preferred_element_type=jnp.float32
    )


def bucket_onehot(distance, first_dist, bucket_ids):
    reached = (distance[None] >= first_dist[:, None, None]).astype(jnp.int32)
    bucket_rows = jnp.sum(reached[1:], axis=0)
    return (bucket_ids[:, None, None] == bucket_rows[None]).astype(jnp.float32)


def per_device(
    inputs,
    segment_ids,
    buckets,
    ln1_gain,
    ln1_bias,
    w_query,
    w_key,
    w_value,
    w_out,
    rel_bias,
    second_norm_gain,
    ln2_bias,
    w_up,
    b_up,
    w_down,
    b_down,
    cotangent,
):
    num_micro, num_rows, local_len, model_width = inputs.shape
    seq_len = segment_ids.shape[2]
    head_count = rel_bias.shape[1]
    head_dim = model_width // head_count
    score_scale = head_dim ** (-0.5)
    num_buckets = rel_bias.shape[0] * lax.axis_size("fsdp")
    num_tokens = num_rows * local_len
    first_pos = lax.axis_index("seq") * local_len
    query_pos = first_pos + jnp.arange(local_len, dtype=jnp.int32)
    key_pos = jnp.arange(seq_len, dtype=jnp.int32)
    distance = query_pos[:, None] - key_pos[None, :]
    causal = distance >= 0
    bucket_ids = jnp.arange(num_buckets, dtype=jnp.int32)
    first_dist = jnp.sum((buckets[None, :] < bucket_ids[:, None]).astype(jnp.int32), axis=1)
    bucket_onehot_matrix = bucket_onehot(distance, first_dist, bucket_ids)
    summed = None
    result_list = []
    grad_list = []
    for micro_step in range(num_micro):
        gathered = (
            lax.all_gather(ln1_gain, "fsdp", axis=0, tiled=True),
            lax.all_gather(ln1_bias, "fsdp", axis=0, tiled=True),
            lax.all_gather(w_query, "fsdp", axis=0, tiled=True),
            lax.all_gather(w_key, "fsdp", axis=0, tiled=True),
            lax.all_gather(w_value, "fsdp", axis=0, tiled=True),
            lax.all_gather(w_out, "fsdp", axis=0, tiled=True),
            lax.all_gather(rel_bias, "fsdp", axis=0, tiled=True),
            lax.all_gather(second_norm_gain, "fsdp", axis=0, tiled=True),
            lax.all_gather(ln2_bias, "fsdp", axis=0, tiled=True),
            lax.all_gather(w_up, "fsdp", axis=0, tiled=True),
            lax.all_gather(b_up, "fsdp", axis=0, tiled=True),
            lax.all_gather(w_down, "fsdp", axis=0, tiled=True),
            lax.all_gather(b_down, "fsdp", axis=0, tiled=True),
        )
        (
            norm1_gain,
            norm1_shift,
            query_mat,
            key_mat,
            value_mat,
            out_mat,
            rel_table,
            norm2_gain,
            norm2_shift,
            up_mat,
            up_bias,
            down_mat,
            down_bias,
        ) = gathered
        relative_float_bias = rel_table.astype(jnp.float32)
        score_position_bias = jnp.einsum(
            "uia,uw->wia", bucket_onehot_matrix, relative_float_bias, precision=EXACT_PRECISION
        )
        row_x = inputs[micro_step].reshape(num_tokens, model_width).astype(jnp.float32)
        normed_one, norm1_pull = jax.vjp(
            layer_norm, row_x, norm1_gain.astype(jnp.float32), norm1_shift.astype(jnp.float32)
        )
        normed_low = normed_one.astype(jnp.bfloat16)
        queries = jnp.dot(normed_low, query_mat, preferred_element_type=jnp.float32).astype(
            jnp.bfloat16
        )
        keys_local = jnp.dot(normed_low, key_mat, preferred_element_type=jnp.float32).astype(
            jnp.bfloat16
        )
        values_local = jnp.dot(normed_low, value_mat, preferred_element_type=jnp.float32).astype(
            jnp.bfloat16
        )
        keys_all, values_all = (
            lax.all_gather(
                keys_local.reshape(num_rows, local_len, model_width), "seq", axis=1, tiled=True
            ),
            lax.all_gather(
                values_local.reshape(num_rows, local_len, model_width), "seq", axis=1, tiled=True
            ),
        )
        row_segment_ids = segment_ids[micro_step]
        query_segs = lax.dynamic_slice_in_dim(row_segment_ids, first_pos, local_len, 1)
        seg_mask = (query_segs[:, :, None] == row_segment_ids[:, None, :]) & causal[None]
        query_four = queries.reshape(num_rows, local_len, head_count, head_dim)
        keys_four = keys_all.reshape(num_rows, seq_len, head_count, head_dim)
        values_four = values_all.reshape(num_rows, seq_len, head_count, head_dim)

        def make_logits():
            raw_scores = (
                jnp.einsum(
                    "rqhd,rkhd->rhqk", query_four, keys_four, preferred_element_type=jnp.float32
                )
                * score_scale
                + score_position_bias[None]
            )
            return jnp.where(seg_mask[:, None], raw_scores, masked_out)

        logits = make_logits()
        row_peak = jnp.max(logits, axis=-1, keepdims=True)
        expo = jnp.exp(logits - row_peak)
        row_total = jnp.sum(expo, axis=-1, keepdims=True)
        soft_probs = expo / row_total
        log_total = row_peak + jnp.log(row_total)
        attended = jnp.einsum(
            "rhqk,rkhd->rqhd",
            soft_probs.astype(jnp.bfloat16),
            values_four,
            preferred_element_type=jnp.float32,
        )
        attended = attended.reshape(num_tokens, model_width).astype(jnp.bfloat16)
        middle = row_x + jnp.dot(attended, out_mat, preferred_element_type=jnp.float32)
        normed_two, norm2_pull = jax.vjp(
            layer_norm, middle, norm2_gain.astype(jnp.float32), norm2_shift.astype(jnp.float32)
        )
        normed_two_low = normed_two.astype(jnp.bfloat16)
        pre_act = jnp.dot(
            normed_two_low, up_mat, preferred_element_type=jnp.float32
        ) + up_bias.astype(jnp.float32)
        activation, gelu_pull = jax.vjp(gelu_exact, pre_act)
        activation_low = activation.astype(jnp.bfloat16)
        result_row = (
            middle
            + jnp.dot(activation_low, down_mat, preferred_element_type=jnp.float32)
            + down_bias.astype(jnp.float32)
        )
        result_list.append(
            result_row.astype(jnp.bfloat16).reshape(num_rows, local_len, model_width)
        )
        grad_out = cotangent[micro_step].reshape(num_tokens, model_width)
        grad_out_f = grad_out.astype(jnp.float32)
        grad_w_down = token_dot(activation_low, grad_out)
        grad_b_down = jnp.sum(grad_out_f, axis=0)
        grad_act = back_dot(grad_out, down_mat)
        grad_pre = gelu_pull(grad_act)[0].astype(jnp.bfloat16)
        grad_b_up = jnp.sum(grad_pre.astype(jnp.float32), axis=0)
        grad_w_up = token_dot(normed_two_low, grad_pre)
        grad_norm2 = back_dot(grad_pre, up_mat)
        grad_mid_norm, grad_ln2_gain, grad_ln2_bias = norm2_pull(grad_norm2)
        grad_middle = grad_out_f + grad_mid_norm
        grad_branch = grad_middle.astype(jnp.bfloat16)
        grad_w_out = token_dot(attended, grad_branch)
        grad_attended = (
            back_dot(grad_branch, out_mat)
            .astype(jnp.bfloat16)
            .reshape(num_rows, local_len, head_count, head_dim)
        )
        again_probs = jnp.exp(make_logits() - log_total)
        grad_probs = jnp.einsum(
            "rqhd,rkhd->rhqk", grad_attended, values_four, preferred_element_type=jnp.float32
        )
        row_delta = jnp.sum(grad_probs * again_probs, axis=-1, keepdims=True)
        grad_scores = (again_probs * (grad_probs - row_delta)).astype(jnp.bfloat16)
        grad_queries = (
            jnp.einsum(
                "rhqk,rkhd->rqhd", grad_scores, keys_four, preferred_element_type=jnp.float32
            )
            * score_scale
        ).astype(jnp.bfloat16)
        grad_rel = jnp.einsum(
            "vlp,glp->vg",
            bucket_onehot_matrix,
            jnp.sum(grad_scores.astype(jnp.float32), axis=0),
            precision=EXACT_PRECISION,
        )
        grad_values = jnp.einsum(
            "rhqk,rqhd->rkhd",
            again_probs.astype(jnp.bfloat16),
            grad_attended,
            preferred_element_type=jnp.float32,
        )
        grad_keys = (
            jnp.einsum(
                "rhqk,rqhd->rkhd", grad_scores, query_four, preferred_element_type=jnp.float32
            )
            * score_scale
        )
        key_grads, value_grads = (
            lax.psum_scatter(
                grad_keys.reshape(num_rows, seq_len, model_width).astype(jnp.bfloat16),
                "seq",
                scatter_dimension=1,
                tiled=True,
            ).astype(jnp.float32),
            lax.psum_scatter(
                grad_values.reshape(num_rows, seq_len, model_width).astype(jnp.bfloat16),
                "seq",
                scatter_dimension=1,
                tiled=True,
            ).astype(jnp.float32),
        )
        key_grads = key_grads.astype(jnp.bfloat16).reshape(num_tokens, model_width)
        value_grads = value_grads.astype(jnp.bfloat16).reshape(num_tokens, model_width)
        grad_queries = grad_queries.reshape(num_tokens, model_width)
        grad_w_query = token_dot(normed_low, grad_queries)
        grad_w_key = token_dot(normed_low, key_grads)
        grad_w_value = token_dot(normed_low, value_grads)
        gradient_first_norm = (
            back_dot(grad_queries, query_mat)
            + back_dot(key_grads, key_mat)
            + back_dot(value_grads, value_mat)
        )
        grad_x_norm, grad_ln1_gain, grad_ln1_bias = norm1_pull(gradient_first_norm)
        grad_list.append(
            (grad_middle + grad_x_norm)
            .astype(jnp.bfloat16)
            .reshape(num_rows, local_len, model_width)
        )
        local_grads = (
            grad_ln1_gain,
            grad_ln1_bias,
            grad_w_query,
            grad_w_key,
            grad_w_value,
            grad_w_out,
            grad_rel,
            grad_ln2_gain,
            grad_ln2_bias,
            grad_w_up,
            grad_b_up,
            grad_w_down,
            grad_b_down,
        )
        shard_part = (
            lax.psum_scatter(
                local_grads[0].astype(jnp.bfloat16), "fsdp", scatter_dimension=0, tiled=True
            ).astype(jnp.float32),
            lax.psum_scatter(
                local_grads[1].astype(jnp.bfloat16), "fsdp", scatter_dimension=0, tiled=True
            ).astype(jnp.float32),
            lax.psum_scatter(
                local_grads[2].astype(jnp.bfloat16), "fsdp", scatter_dimension=0, tiled=True
            ).astype(jnp.float32),
            lax.psum_scatter(
                local_grads[3].astype(jnp.bfloat16), "fsdp", scatter_dimension=0, tiled=True
            ).astype(jnp.float32),
            lax.psum_scatter(
                local_grads[4].astype(jnp.bfloat16), "fsdp", scatter_dimension=0, tiled=True
            ).astype(jnp.float32),
            lax.psum_scatter(
                local_grads[5].astype(jnp.bfloat16), "fsdp", scatter_dimension=0, tiled=True
            ).astype(jnp.float32),
            lax.psum_scatter(
                local_grads[6].astype(jnp.bfloat16), "fsdp", scatter_dimension=0, tiled=True
            ).astype(jnp.float32),
            lax.psum_scatter(
                local_grads[7].astype(jnp.bfloat16), "fsdp", scatter_dimension=0, tiled=True
            ).astype(jnp.float32),
            lax.psum_scatter(
                local_grads[8].astype(jnp.bfloat16), "fsdp", scatter_dimension=0, tiled=True
            ).astype(jnp.float32),
            lax.psum_scatter(
                local_grads[9].astype(jnp.bfloat16), "fsdp", scatter_dimension=0, tiled=True
            ).astype(jnp.float32),
            lax.psum_scatter(
                local_grads[10].astype(jnp.bfloat16), "fsdp", scatter_dimension=0, tiled=True
            ).astype(jnp.float32),
            lax.psum_scatter(
                local_grads[11].astype(jnp.bfloat16), "fsdp", scatter_dimension=0, tiled=True
            ).astype(jnp.float32),
            lax.psum_scatter(
                local_grads[12].astype(jnp.bfloat16), "fsdp", scatter_dimension=0, tiled=True
            ).astype(jnp.float32),
        )
        summed = shard_part if summed is None else jax.tree.map(jnp.add, summed, shard_part)
    totals = (
        lax.psum(summed[0].astype(jnp.bfloat16), "seq").astype(jnp.float32),
        lax.psum(summed[1].astype(jnp.bfloat16), "seq").astype(jnp.float32),
        lax.psum(summed[2].astype(jnp.bfloat16), "seq").astype(jnp.float32),
        lax.psum(summed[3].astype(jnp.bfloat16), "seq").astype(jnp.float32),
        lax.psum(summed[4].astype(jnp.bfloat16), "seq").astype(jnp.float32),
        lax.psum(summed[5].astype(jnp.bfloat16), "seq").astype(jnp.float32),
        lax.psum(summed[6].astype(jnp.bfloat16), "seq").astype(jnp.float32),
        lax.psum(summed[7].astype(jnp.bfloat16), "seq").astype(jnp.float32),
        lax.psum(summed[8].astype(jnp.bfloat16), "seq").astype(jnp.float32),
        lax.psum(summed[9].astype(jnp.bfloat16), "seq").astype(jnp.float32),
        lax.psum(summed[10].astype(jnp.bfloat16), "seq").astype(jnp.float32),
        lax.psum(summed[11].astype(jnp.bfloat16), "seq").astype(jnp.float32),
        lax.psum(summed[12].astype(jnp.bfloat16), "seq").astype(jnp.float32),
    )
    return (
        jnp.stack(result_list),
        jnp.stack(grad_list),
        totals[0],
        totals[1],
        totals[2],
        totals[3],
        totals[4],
        totals[5],
        totals[6],
        totals[7],
        totals[8],
        totals[9],
        totals[10],
        totals[11],
        totals[12],
    )


def solution(mesh):
    return jax.shard_map(
        per_device,
        mesh=mesh,
        in_specs=(
            P(None, "fsdp", "seq", None),
            P(None, "fsdp", None),
            P(),
            P("fsdp"),
            P("fsdp"),
            P("fsdp", None),
            P("fsdp", None),
            P("fsdp", None),
            P("fsdp", None),
            P("fsdp", None),
            P("fsdp"),
            P("fsdp"),
            P("fsdp", None),
            P("fsdp"),
            P("fsdp", None),
            P("fsdp"),
            P(None, "fsdp", "seq", None),
        ),
        out_specs=(
            P(None, "fsdp", "seq", None),
            P(None, "fsdp", "seq", None),
            P("fsdp"),
            P("fsdp"),
            P("fsdp", None),
            P("fsdp", None),
            P("fsdp", None),
            P("fsdp", None),
            P("fsdp", None),
            P("fsdp"),
            P("fsdp"),
            P("fsdp", None),
            P("fsdp"),
            P("fsdp", None),
            P("fsdp"),
        ),
        check_vma=False,
    )
```

profile of v0, /device:TPU:0, one launch (start us, length us, event | category | flops | bytes accessed | tf_op | source)
XLA Modules:
  0.0 2055.5 jit_solution(9363248587604546310)
XLA Ops:
  9.5 10.3 all-gather.6
  19.8 8.6 all-gather.7
  32.4 8.1 all-gather.30.cloned.1.call-done
  47.2 23.2 %all-gather.26.cloned.1.call-done = bf16[1024,1024]{1,0:T(8,128)(2,1)} async-done(((bf16[128,1024]{1,0:T(8,128)(2,1)}), bf16[1024,1024]{1,0:T(8,128)(2,1)}) %all-gather.26.cloned.1.call-update) | async-done | bytes 2097168 | tf_op jit(solution)/shard_map/all_gather | solution.py:82
  79.1 8.7 all-gather.9
  87.8 7.8 all-gather.10
  95.6 8.8 all-gather.8
  104.5 8.2 all-gather.11
  116.1 9.2 fusion.3
  132.6 15.6 all-gather.48.cloned.1.call-done
  151.0 22.0 %fusion.231 = (f32[16,256]{1,0:T(8,128)S(1)}, f32[16,256,1024]{2,1,0:T(8,128)}) fusion(f32[256,1024,16]{1,2,0:T(8,128)} %fusion.3, bf16[256,16,64]{0,2,1:T(8,128)(2,1)S(1)} %bitcast.439, bf16[1024,16,64]{0,2,1:T(8,128)(2,1)S(1)} %bitcast.428, pred[256,1024]{1,0:T(8,128)(4,1)S(1)} %get-tuple-element.107), kind=kOutput, calls=%fused_computation.386 | convolution fusion | flops 553644032 | bytes 36454400 | tf_op jit(solution)/shard_map/rqhd,rkhd->rhqk/dot_general | solution.py:142
  180.8 14.1 all-gather.40.cloned.1.call-done
  197.7 43.8 %all-gather.46.cloned.1.call-done = bf16[1024,1024]{1,0:T(8,128)(2,1)} async-done(((bf16[256,1024]{1,0:T(8,128)(2,1)}), bf16[1024,1024]{1,0:T(8,128)(2,1)}) %all-gather.46.cloned.1.call-update) | async-done | bytes 2097168 | tf_op jit(solution)/shard_map/all_gather | solution.py:129
  245.5 42.9 %all-gather.38.cloned.1.call-done = bf16[1024,1024]{1,0:T(8,128)(2,1)} async-done(((bf16[256,1024]{1,0:T(8,128)(2,1)}), bf16[1024,1024]{1,0:T(8,128)(2,1)}) %all-gather.38.cloned.1.call-update) | async-done | bytes 2097168 | tf_op jit(solution)/shard_map/all_gather | solution.py:129
  292.3 9.2 fusion.83
  301.5 15.4 all-gather.32.cloned.1.call-done
  319.9 21.5 %fusion.233 = (f32[16,256]{1,0:T(8,128)S(1)}, f32[16,256,1024]{2,1,0:T(8,128)}) fusion(f32[256,1024,16]{1,2,0:T(8,128)} %fusion.3, bf16[256,16,64]{0,2,1:T(8,128)(2,1)S(1)} %bitcast.437, bf16[1024,16,64]{0,2,1:T(8,128)(2,1)S(1)} %bitcast.430, pred[256,1024]{1,0:T(8,128)(4,1)S(1)} %get-tuple-element.108), kind=kOutput, calls=%fused_computation.388 | convolution fusion | flops 553644032 | bytes 36454400 | tf_op jit(solution)/shard_map/rqhd,rkhd->rhqk/dot_general | solution.py:142
  341.4 9.2 fusion.11
  362.6 10.6 all-gather.34.cloned.1.call-done
  373.2 16.4 multiply_convert_fusion.6
  389.6 16.5 multiply_convert_fusion.8
  406.1 23.3 %all-gather.36.cloned.1.call-done = bf16[4096,1024]{1,0:T(8,128)(2,1)} async-done(((bf16[512,1024]{1,0:T(8,128)(2,1)}), bf16[4096,1024]{1,0:T(8,128)(2,1)}) %all-gather.36.cloned.1.call-update) | async-done | bytes 8388624 | tf_op jit(solution)/shard_map/all_gather | solution.py:89
  429.4 12.4 fusion.239
  448.7 11.7 fusion.237
  471.5 15.1 multiply_reduce_fusion
  488.6 7.9 multiply_convert_fusion
  500.5 9.1 fusion.56
  513.3 14.6 multiply_reduce_fusion.2
  530.4 7.8 multiply_convert_fusion.2
  542.3 9.2 fusion.50
  571.7 18.2 reduce-scatter.35.cloned.1.call-done
  593.6 41.8 %reduce-scatter.25.cloned.1.call-done = bf16[1,256,1024]{1,2,0:T(8,128)(2,1)} async-done(((bf16[1,1024,1024]{1,2,0:T(8,128)(2,1)}), bf16[1,256,1024]{1,2,0:T(8,128)(2,1)}) %reduce-scatter.25.cloned.1.call-update) | async-done | bytes 524304 | tf_op jit(solution)/shard_map/reduce_scatter | solution.py:230
  638.9 42.0 %reduce-scatter.27.cloned.1.call-done = bf16[1,256,1024]{1,2,0:T(8,128)(2,1)} async-done(((bf16[1,1024,1024]{1,2,0:T(8,128)(2,1)}), bf16[1,256,1024]{1,2,0:T(8,128)(2,1)}) %reduce-scatter.27.cloned.1.call-update) | async-done | bytes 524304 | tf_op jit(solution)/shard_map/reduce_scatter | solution.py:236
  693.6 39.5 %all-gather.44.cloned.1.call-done = bf16[1024,1024]{1,0:T(8,128)(2,1)} async-done(((bf16[256,1024]{1,0:T(8,128)(2,1)}), bf16[1024,1024]{1,0:T(8,128)(2,1)}) %all-gather.44.cloned.1.call-update) | async-done | bytes 2097168 | tf_op jit(solution)/shard_map/all_gather | solution.py:126
  736.4 22.1 %fusion.235 = (f32[16,256]{1,0:T(8,128)S(1)}, f32[16,256,1024]{2,1,0:T(8,128)}) fusion(f32[256,1024,16]{1,2,0:T(8,128)} %fusion.3, bf16[256,16,64]{0,2,1:T(8,128)(2,1)S(1)} %bitcast.441, bf16[1024,16,64]{0,2,1:T(8,128)(2,1)S(1)} %bitcast.432, pred[256,1024]{1,0:T(8,128)(4,1)S(1)} %copy-done.49), kind=kOutput, calls=%fused_computation.390 | convolution fusion | flops 553644032 | bytes 36454400 | tf_op jit(solution)/shard_map/rqhd,rkhd->rhqk/dot_general | solution.py:142
  766.3 13.5 all-gather.42.cloned.1.call-done
  782.7 8.3 fusion.84
  793.5 16.4 multiply_convert_fusion.7
  827.4 9.2 fusion.53
  836.6 10.0 multiply_reduce_fusion.1
  846.6 7.8 multiply_convert_fusion.1
  897.1 27.6 %reduce-scatter.29.cloned.1.call-done = bf16[1,256,1024]{1,2,0:T(8,128)(2,1)} async-done(((bf16[1,1024,1024]{1,2,0:T(8,128)(2,1)}), bf16[1,256,1024]{1,2,0:T(8,128)(2,1)}) %reduce-scatter.29.cloned.1.call-update) | async-done | bytes 524304 | tf_op jit(solution)/shard_map/reduce_scatter | solution.py:230
  936.5 7.9 convolution_convert_fusion.5
  979.4 8.6 all-gather.12
  1025.6 7.9 fusion.107
  1033.5 24.4 %reduce-scatter.57.cloned.1.call-done = bf16[128,1024]{1,0:T(8,128)(2,1)} async-done(((bf16[1024,1024]{1,0:T(8,128)(2,1)}), bf16[128,1024]{1,0:T(8,128)(2,1)}) %reduce-scatter.57.cloned.1.call-update) | async-done | bytes 262160 | tf_op jit(solution)/shard_map/reduce_scatter | solution.py:291
  1059.8 42.9 %reduce-scatter.41.cloned.1.call-done = bf16[128,1024]{1,0:T(8,128)(2,1)} async-done(((bf16[1024,1024]{1,0:T(8,128)(2,1)}), bf16[128,1024]{1,0:T(8,128)(2,1)}) %reduce-scatter.41.cloned.1.call-update) | async-done | bytes 262160 | tf_op jit(solution)/shard_map/reduce_scatter | solution.py:282
  1102.7 44.5 %reduce-scatter.37.cloned.1.call-done = bf16[128,1024]{1,0:T(8,128)(2,1)} async-done(((bf16[1024,1024]{1,0:T(8,128)(2,1)}), bf16[128,1024]{1,0:T(8,128)(2,1)}) %reduce-scatter.37.cloned.1.call-update) | async-done | bytes 262160 | tf_op jit(solution)/shard_map/reduce_scatter | solution.py:282
  1147.2 44.7 %reduce-scatter.39.cloned.1.call-done = bf16[128,1024]{1,0:T(8,128)(2,1)} async-done(((bf16[1024,1024]{1,0:T(8,128)(2,1)}), bf16[128,1024]{1,0:T(8,128)(2,1)}) %reduce-scatter.39.cloned.1.call-update) | async-done | bytes 262160 | tf_op jit(solution)/shard_map/reduce_scatter | solution.py:282
  1197.7 38.8 %reduce-scatter.49.cloned.1.call-done = bf16[128,1024]{1,0:T(8,128)(2,1)} async-done(((bf16[1024,1024]{1,0:T(8,128)(2,1)}), bf16[128,1024]{1,0:T(8,128)(2,1)}) %reduce-scatter.49.cloned.1.call-update) | async-done | bytes 262160 | tf_op jit(solution)/shard_map/reduce_scatter | solution.py:288
  1236.5 44.7 %reduce-scatter.53.cloned.1.call-done = bf16[128,1024]{1,0:T(8,128)(2,1)} async-done(((bf16[1024,1024]{1,0:T(8,128)(2,1)}), bf16[128,1024]{1,0:T(8,128)(2,1)}) %reduce-scatter.53.cloned.1.call-update) | async-done | bytes 262160 | tf_op jit(solution)/shard_map/reduce_scatter | solution.py:288
  1281.3 44.4 %reduce-scatter.51.cloned.1.call-done = bf16[128,1024]{1,0:T(8,128)(2,1)} async-done(((bf16[1024,1024]{1,0:T(8,128)(2,1)}), bf16[128,1024]{1,0:T(8,128)(2,1)}) %reduce-scatter.51.cloned.1.call-update) | async-done | bytes 262160 | tf_op jit(solution)/shard_map/reduce_scatter | solution.py:288
  1327.6 43.0 %reduce-scatter.47.cloned.1.call-done = bf16[128,1024]{1,0:T(8,128)(2,1)} async-done(((bf16[1024,1024]{1,0:T(8,128)(2,1)}), bf16[128,1024]{1,0:T(8,128)(2,1)}) %reduce-scatter.47.cloned.1.call-update) | async-done | bytes 262160 | tf_op jit(solution)/shard_map/reduce_scatter | solution.py:285
  1370.5 44.5 %reduce-scatter.43.cloned.1.call-done = bf16[128,1024]{1,0:T(8,128)(2,1)} async-done(((bf16[1024,1024]{1,0:T(8,128)(2,1)}), bf16[128,1024]{1,0:T(8,128)(2,1)}) %reduce-scatter.43.cloned.1.call-update) | async-done | bytes 262160 | tf_op jit(solution)/shard_map/reduce_scatter | solution.py:285
  1415.1 44.7 %reduce-scatter.45.cloned.1.call-done = bf16[128,1024]{1,0:T(8,128)(2,1)} async-done(((bf16[1024,1024]{1,0:T(8,128)(2,1)}), bf16[128,1024]{1,0:T(8,128)(2,1)}) %reduce-scatter.45.cloned.1.call-update) | async-done | bytes 262160 | tf_op jit(solution)/shard_map/reduce_scatter | solution.py:285
  1461.7 72.8 %reduce-scatter.65.cloned.1.call-done = bf16[128,4096]{1,0:T(8,128)(2,1)} async-done(((bf16[1024,4096]{1,0:T(8,128)(2,1)}), bf16[128,4096]{1,0:T(8,128)(2,1)}) %reduce-scatter.65.cloned.1.call-update) | async-done | bytes 1048592 | tf_op jit(solution)/shard_map/reduce_scatter | solution.py:303
  1534.6 75.2 %reduce-scatter.61.cloned.1.call-done = bf16[128,4096]{1,0:T(8,128)(2,1)} async-done(((bf16[1024,4096]{1,0:T(8,128)(2,1)}), bf16[128,4096]{1,0:T(8,128)(2,1)}) %reduce-scatter.61.cloned.1.call-update) | async-done | bytes 1048592 | tf_op jit(solution)/shard_map/reduce_scatter | solution.py:303
  1609.8 74.6 %reduce-scatter.63.cloned.1.call-done = bf16[128,4096]{1,0:T(8,128)(2,1)} async-done(((bf16[1024,4096]{1,0:T(8,128)(2,1)}), bf16[128,4096]{1,0:T(8,128)(2,1)}) %reduce-scatter.63.cloned.1.call-update) | async-done | bytes 1048592 | tf_op jit(solution)/shard_map/reduce_scatter | solution.py:303
  1687.7 71.9 %reduce-scatter.71.cloned.1.call-done = bf16[512,1024]{1,0:T(8,128)(2,1)} async-done(((bf16[4096,1024]{1,0:T(8,128)(2,1)}), bf16[512,1024]{1,0:T(8,128)(2,1)}) %reduce-scatter.71.cloned.1.call-update) | async-done | bytes 1048592 | tf_op jit(solution)/shard_map/reduce_scatter | solution.py:309
  1759.6 74.8 %reduce-scatter.67.cloned.1.call-done = bf16[512,1024]{1,0:T(8,128)(2,1)} async-done(((bf16[4096,1024]{1,0:T(8,128)(2,1)}), bf16[512,1024]{1,0:T(8,128)(2,1)}) %reduce-scatter.67.cloned.1.call-update) | async-done | bytes 1048592 | tf_op jit(solution)/shard_map/reduce_scatter | solution.py:309
  1834.3 75.0 %reduce-scatter.69.cloned.1.call-done = bf16[512,1024]{1,0:T(8,128)(2,1)} async-done(((bf16[4096,1024]{1,0:T(8,128)(2,1)}), bf16[512,1024]{1,0:T(8,128)(2,1)}) %reduce-scatter.69.cloned.1.call-update) | async-done | bytes 1048592 | tf_op jit(solution)/shard_map/reduce_scatter | solution.py:309
  1919.6 25.7 %all-reduce.21 = (bf16[1024]{0:T(1024)(128)(2,1)S(1)}, bf16[1024]{0:T(1024)(128)(2,1)S(1)}, bf16[1024]{0:T(1024)(128)(2,1)S(1)}, bf16[1024]{0:T(1024)(128)(2,1)S...) all-reduce(bf16[1024]{0:T(1024)(128)(2,1)S(1)} %get-tuple-element.1, ...), channel_id=16, replica_groups=mesh['fsdp'=8,'seq'=4] {'fsdp'}, use_global_device_ids=true, to_apply=%region_46.47.clone | all-reduce | flops 29184 | bytes 116736
  1945.9 12.8 all-reduce.22
  1966.4 70.2 %all-reduce.26.cloned.1.call-done = (bf16[128,1024]{1,0:T(8,128)(2,1)}, bf16[128,1024]{1,0:T(8,128)(2,1)}, bf16[128,1024]{1,0:T(8,128)(2,1)}, bf16[128,1024]{1,0...) async-done(((bf16[128,1024]{1,0:T(8,128)(2,1)}, bf16[128,1024]{1,0:T(8,128)(2,1)}, bf16[128,1024]{1,0:T(8,128)(2,1)}, bf16[128,1024]{1,0:T(8,128)(2,1)}, ...) | async-done | bytes 3145744 | tf_op jit(solution)/shard_map/psum | solution.py:320
  (583 shorter events, 344.7 us)
Async XLA Ops:
  7.2 33.4 %all-gather.30.cloned.1.call-start = ((), (), s32[]{:S(2)}) async-start(), calls=%async_computation.26 | async-start | bytes 2359296 | tf_op jit(solution)/shard_map/all_gather | solution.py:81
  7.9 62.4 %all-gather.26.cloned.1.call-start = ((), (), s32[]{:S(2)}) async-start(), calls=%async_computation.24 | async-start | bytes 2359296 | tf_op jit(solution)/shard_map/all_gather | solution.py:82
  8.7 117.9 %all-gather.28.cloned.1.call-start = ((), (), s32[]{:S(2)}) async-start(), calls=%async_computation.25 | async-start | bytes 2359296 | tf_op jit(solution)/shard_map/all_gather | solution.py:80
  9.4 138.7 %all-gather.48.cloned.1.call-start = ((), (), s32[]{:S(2)}) async-start(), calls=%async_computation.59 | async-start | bytes 2621440 | tf_op jit(solution)/shard_map/all_gather | solution.py:126
  19.8 110.2 %copy-start.82 = (f32[8,1,128]{2,1,0:T(1,128)}, f32[8,1,128]{2,1,0:T(1,128)S(1)}, u32[]{:S(2)}) copy-start(f32[8,1,128]{2,1,0:T(1,128)S(1)} %convert_element_type.938) | copy-start | bytes 12292
  28.4 101.6 %copy-start.135 = (f32[8,1,128]{2,1,0:T(1,128)}, f32[8,1,128]{2,1,0:T(1,128)S(1)}, u32[]{:S(2)}) copy-start(f32[8,1,128]{2,1,0:T(1,128)S(1)} %convert_element_type.939) | copy-start | bytes 12292
  30.6 96.0 %copy-start.107 = (f32[256]{0:T(256)}, f32[256]{0:T(256)S(1)}, u32[]{:S(2)}) copy-start(f32[256]{0:T(256)S(1)} %get-tuple-element.141) | copy-start | bytes 3076
  30.6 99.4 %copy-start.111 = (f32[256]{0:T(256)}, f32[256]{0:T(256)S(1)}, u32[]{:S(2)}) copy-start(f32[256]{0:T(256)S(1)} %get-tuple-element.140) | copy-start | bytes 3076
  32.4 97.6 %copy-start.129 = (f32[256]{0:T(256)}, f32[256]{0:T(256)S(1)}, u32[]{:S(2)}) copy-start(f32[256]{0:T(256)S(1)} %fusion.186) | copy-start | bytes 3076
  43.9 151.0 %all-gather.40.cloned.1.call-start = ((), (), s32[]{:S(2)}) async-start(), calls=%async_computation.55 | async-start | bytes 2621440 | tf_op jit(solution)/shard_map/all_gather | solution.py:126
  44.0 82.7 %copy-start.126 = (f32[256]{0:T(256)}, f32[256]{0:T(256)S(1)}, u32[]{:S(2)}) copy-start(f32[256]{0:T(256)S(1)} %fusion.182) | copy-start | bytes 3076
  47.1 194.4 %all-gather.46.cloned.1.call-start = ((), (), s32[]{:S(2)}) async-start(), calls=%async_computation.58 | async-start | bytes 2621440 | tf_op jit(solution)/shard_map/all_gather | solution.py:129
  73.6 214.8 %all-gather.38.cloned.1.call-start = ((), (), s32[]{:S(2)}) async-start(), calls=%async_computation.54 | async-start | bytes 2621440 | tf_op jit(solution)/shard_map/all_gather | solution.py:129
  76.8 240.1 %all-gather.32.cloned.1.call-start = ((), (), s32[]{:S(2)}) async-start(), calls=%async_computation.27 | async-start | bytes 2359296 | tf_op jit(solution)/shard_map/all_gather | solution.py:83
  77.5 295.7 %all-gather.34.cloned.1.call-start = ((), (), s32[]{:S(2)}) async-start(), calls=%async_computation.28 | async-start | bytes 9437184 | tf_op jit(solution)/shard_map/all_gather | solution.py:87
  78.3 351.1 %all-gather.36.cloned.1.call-start = ((), (), s32[]{:S(2)}) async-start(), calls=%async_computation.29 | async-start | bytes 9437184 | tf_op jit(solution)/shard_map/all_gather | solution.py:89
  78.8 489.5 %reduce-scatter.33.cloned.1.call-start = ((), (), s32[]{:S(2)}) async-start(), calls=%async_computation.34 | async-start | bytes 2621440 | tf_op jit(solution)/shard_map/reduce_scatter | solution.py:230
  95.6 293.9 %copy-start.71 = (f32[8,1,128]{2,1,0:T(1,128)}, f32[8,1,128]{2,1,0:T(1,128)S(1)}, u32[]{:S(2)}) copy-start(f32[8,1,128]{2,1,0:T(1,128)S(1)} %convert_element_type.941) | copy-start | bytes 12292
  112.7 276.9 %copy-start.92 = (f32[8,1,512]{2,1,0:T(1,128)}, f32[8,1,512]{2,1,0:T(1,128)S(1)}, u32[]{:S(2)}) copy-start(f32[8,1,512]{2,1,0:T(1,128)S(1)} %convert_element_type.942) | copy-start | bytes 49156
  197.7 122.2 %copy-start.6 = (bf16[1024,1024]{0,1:T(8,128)(2,1)}, bf16[1024,1024]{0,1:T(8,128)(2,1)S(1)}, u32[]{:S(2)}) copy-start(bf16[1024,1024]{0,1:T(8,128)(2,1)S(1)} %copy.97) | copy-start | bytes 6291460
  319.6 148.4 %copy-start.18 = (f32[256,1024]{1,0:T(8,128)}, f32[256,1024]{1,0:T(8,128)S(1)}, u32[]{:S(2)}) copy-start(f32[256,1024]{1,0:T(8,128)S(1)} %get-tuple-element.112) | copy-start | bytes 3145732
  319.6 148.4 %copy-start.86 = (f32[256]{0:T(256)}, f32[256]{0:T(256)S(1)}, u32[]{:S(2)}) copy-start(f32[256]{0:T(256)S(1)} %broadcast_multiply_fusion) | copy-start | bytes 3076
  360.7 107.3 %copy-start.88 = (f32[256]{0:T(256)}, f32[256]{0:T(256)S(1)}, u32[]{:S(2)}) copy-start(f32[256]{0:T(256)S(1)} %broadcast_multiply_fusion.4) | copy-start | bytes 3076
  362.0 106.0 %copy-start.96 = (f32[256]{0:T(256)}, f32[256]{0:T(256)S(1)}, u32[]{:S(2)}) copy-start(f32[256]{0:T(256)S(1)} %fusion.187) | copy-start | bytes 3076
  362.0 106.0 %copy-start.94 = (f32[256]{0:T(256)}, f32[256]{0:T(256)S(1)}, u32[]{:S(2)}) copy-start(f32[256]{0:T(256)S(1)} %fusion.183) | copy-start | bytes 3076
  500.4 89.4 %reduce-scatter.35.cloned.1.call-start = ((), (), s32[]{:S(2)}) async-start(), calls=%async_computation.35 | async-start | bytes 2621440 | tf_op jit(solution)/shard_map/reduce_scatter | solution.py:236
  509.7 125.7 %reduce-scatter.25.cloned.1.call-start = ((), (), s32[]{:S(2)}) async-start(), calls=%async_computation.30 | async-start | bytes 2621440 | tf_op jit(solution)/shard_map/reduce_scatter | solution.py:230
  542.2 138.6 %reduce-scatter.27.cloned.1.call-start = ((), (), s32[]{:S(2)}) async-start(), calls=%async_computation.31 | async-start | bytes 2621440 | tf_op jit(solution)/shard_map/reduce_scatter | solution.py:236
  551.5 181.6 %all-gather.44.cloned.1.call-start = ((), (), s32[]{:S(2)}) async-start(), calls=%async_computation.57 | async-start | bytes 2621440 | tf_op jit(solution)/shard_map/all_gather | solution.py:126
  551.8 139.2 %copy-start.99 = (f32[256]{0:T(256)}, f32[256]{0:T(256)S(1)}, u32[]{:S(2)}) copy-start(f32[256]{0:T(256)S(1)} %broadcast_multiply_fusion.3) | copy-start | bytes 3076
  571.7 109.2 %copy-start.11 = (bf16[3,1,256,1024]{3,2,1,0:T(8,128)(2,1)S(1)}, bf16[3,1,256,1024]{3,2,1,0:T(8,128)(2,1)}, u32[]{:S(2)}) copy-start(bf16[3,1,256,1024]{3,2,1,0:T(8,128)(2,1)} %param.17) | copy-start | bytes 4718596
  571.7 109.2 %copy-start.83 = (f32[8,1,128]{2,1,0:T(1,128)S(1)}, f32[8,1,128]{2,1,0:T(1,128)}, u32[]{:S(2)}) copy-start(f32[8,1,128]{2,1,0:T(1,128)} %copy-done.82) | copy-start | bytes 12292
  571.7 109.2 %copy-start.108 = (f32[256]{0:T(256)S(1)}, f32[256]{0:T(256)}, u32[]{:S(2)}) copy-start(f32[256]{0:T(256)} %copy-done.107) | copy-start | bytes 3076
  571.7 109.2 %copy-start.112 = (f32[256]{0:T(256)S(1)}, f32[256]{0:T(256)}, u32[]{:S(2)}) copy-start(f32[256]{0:T(256)} %copy-done.111) | copy-start | bytes 3076
  687.7 92.1 %all-gather.42.cloned.1.call-start = ((), (), s32[]{:S(2)}) async-start(), calls=%async_computation.56 | async-start | bytes 2621440 | tf_op jit(solution)/shard_map/all_gather | solution.py:129
  690.9 197.3 %reduce-scatter.31.cloned.1.call-start = ((), (), s32[]{:S(2)}) async-start(), calls=%async_computation.33 | async-start | bytes 2621440 | tf_op jit(solution)/shard_map/reduce_scatter | solution.py:236
  693.6 65.0 %copy-start.35 = (bf16[256,1024]{0,1:T(8,128)(2,1)}, bf16[256,1024]{0,1:T(8,128)(2,1)S(1)}, u32[]{:S(2)}) copy-start(bf16[256,1024]{0,1:T(8,128)(2,1)S(1)} %copy.101) | copy-start | bytes 1572868
  766.3 61.0 %copy-start.76 = (f32[16,256]{1,0:T(8,128)}, f32[16,256]{1,0:T(8,128)S(1)}, u32[]{:S(2)}) copy-start(f32[16,256]{1,0:T(8,128)S(1)} %log_add_fusion.1) | copy-start | bytes 49156
  793.1 151.4 %copy-start.16 = (f32[256,1024]{1,0:T(8,128)}, f32[256,1024]{1,0:T(8,128)S(1)}, u32[]{:S(2)}) copy-start(f32[256,1024]{1,0:T(8,128)S(1)} %get-tuple-element.128) | copy-start | bytes 3145732
  836.6 88.2 %reduce-scatter.29.cloned.1.call-start = ((), (), s32[]{:S(2)}) async-start(), calls=%async_computation.32 | async-start | bytes 2621440 | tf_op jit(solution)/shard_map/reduce_scatter | solution.py:230
  858.5 175.0 %reduce-scatter.55.cloned.1.call-start = ((), (), s32[]{:S(2)}) async-start(), calls=%async_computation.45 | async-start | bytes 2359296 | tf_op jit(solution)/shard_map/reduce_scatter | solution.py:291
  860.6 172.9 %reduce-scatter.59.cloned.1.call-start = ((), (), s32[]{:S(2)}) async-start(), calls=%async_computation.47 | async-start | bytes 2359296 | tf_op jit(solution)/shard_map/reduce_scatter | solution.py:291
  862.8 195.1 %reduce-scatter.57.cloned.1.call-start = ((), (), s32[]{:S(2)}) async-start(), calls=%async_computation.46 | async-start | bytes 2359296 | tf_op jit(solution)/shard_map/reduce_scatter | solution.py:291
  864.9 237.8 %reduce-scatter.41.cloned.1.call-start = ((), (), s32[]{:S(2)}) async-start(), calls=%async_computation.38 | async-start | bytes 2359296 | tf_op jit(solution)/shard_map/reduce_scatter | solution.py:282
  868.2 279.0 %reduce-scatter.37.cloned.1.call-start = ((), (), s32[]{:S(2)}) async-start(), calls=%async_computation.36 | async-start | bytes 2359296 | tf_op jit(solution)/shard_map/reduce_scatter | solution.py:282
  871.9 320.1 %reduce-scatter.39.cloned.1.call-start = ((), (), s32[]{:S(2)}) async-start(), calls=%async_computation.37 | async-start | bytes 2359296 | tf_op jit(solution)/shard_map/reduce_scatter | solution.py:282
  882.5 354.0 %reduce-scatter.49.cloned.1.call-start = ((), (), s32[]{:S(2)}) async-start(), calls=%async_computation.42 | async-start | bytes 2359296 | tf_op jit(solution)/shard_map/reduce_scatter | solution.py:288
  885.9 395.4 %reduce-scatter.53.cloned.1.call-start = ((), (), s32[]{:S(2)}) async-start(), calls=%async_computation.44 | async-start | bytes 2359296 | tf_op jit(solution)/shard_map/reduce_scatter | solution.py:288
  888.2 437.5 %reduce-scatter.51.cloned.1.call-start = ((), (), s32[]{:S(2)}) async-start(), calls=%async_computation.43 | async-start | bytes 2359296 | tf_op jit(solution)/shard_map/reduce_scatter | solution.py:288
  891.5 479.0 %reduce-scatter.47.cloned.1.call-start = ((), (), s32[]{:S(2)}) async-start(), calls=%async_computation.41 | async-start | bytes 2359296 | tf_op jit(solution)/shard_map/reduce_scatter | solution.py:285
  893.8 521.3 %reduce-scatter.43.cloned.1.call-start = ((), (), s32[]{:S(2)}) async-start(), calls=%async_computation.39 | async-start | bytes 2359296 | tf_op jit(solution)/shard_map/reduce_scatter | solution.py:285
  897.1 562.7 %reduce-scatter.45.cloned.1.call-start = ((), (), s32[]{:S(2)}) async-start(), calls=%async_computation.40 | async-start | bytes 2359296 | tf_op jit(solution)/shard_map/reduce_scatter | solution.py:285
  928.0 606.6 %reduce-scatter.65.cloned.1.call-start = ((), (), s32[]{:S(2)}) async-start(), calls=%async_computation.50 | async-start | bytes 9437184 | tf_op jit(solution)/shard_map/reduce_scatter | solution.py:303
  935.8 673.9 %reduce-scatter.61.cloned.1.call-start = ((), (), s32[]{:S(2)}) async-start(), calls=%async_computation.48 | async-start | bytes 9437184 | tf_op jit(solution)/shard_map/reduce_scatter | solution.py:303
  944.4 740.0 %reduce-scatter.63.cloned.1.call-start = ((), (), s32[]{:S(2)}) async-start(), calls=%async_computation.49 | async-start | bytes 9437184 | tf_op jit(solution)/shard_map/reduce_scatter | solution.py:303
  952.5 807.0 %reduce-scatter.71.cloned.1.call-start = ((), (), s32[]{:S(2)}) async-start(), calls=%async_computation.53 | async-start | bytes 9437184 | tf_op jit(solution)/shard_map/reduce_scatter | solution.py:309
  961.3 873.1 %reduce-scatter.67.cloned.1.call-start = ((), (), s32[]{:S(2)}) async-start(), calls=%async_computation.51 | async-start | bytes 9437184 | tf_op jit(solution)/shard_map/reduce_scatter | solution.py:309
  968.8 940.6 %reduce-scatter.69.cloned.1.call-start = ((), (), s32[]{:S(2)}) async-start(), calls=%async_computation.52 | async-start | bytes 9437184 | tf_op jit(solution)/shard_map/reduce_scatter | solution.py:309
  976.2 1060.4 %all-reduce.26.cloned.1.call-start = ((), (), s32[]{:S(2)}) async-start(), calls=%async_computation.60 | async-start | bytes 6291456 | tf_op jit(solution)/shard_map/psum | solution.py:320
  1687.7 225.2 %copy-start.101 = (f32[256]{0:T(256)S(1)}, f32[256]{0:T(256)}, u32[]{:S(2)}) copy-start(f32[256]{0:T(256)} %copy-done.99) | copy-start | bytes 3076
  1687.7 225.2 %copy-start.110 = (f32[256]{0:T(256)S(1)}, f32[256]{0:T(256)}, u32[]{:S(2)}) copy-start(f32[256]{0:T(256)} %copy-done.107) | copy-start | bytes 3076
  1687.7 225.2 %copy-start.114 = (f32[256]{0:T(256)S(1)}, f32[256]{0:T(256)}, u32[]{:S(2)}) copy-start(f32[256]{0:T(256)} %copy-done.111) | copy-start | bytes 3076
  1687.7 225.2 %copy-start.128 = (f32[256]{0:T(256)S(1)}, f32[256]{0:T(256)}, u32[]{:S(2)}) copy-start(f32[256]{0:T(256)} %copy-done.126) | copy-start | bytes 3076
  1687.7 225.2 %copy-start.131 = (f32[256]{0:T(256)S(1)}, f32[256]{0:T(256)}, u32[]{:S(2)}) copy-start(f32[256]{0:T(256)} %copy-done.129) | copy-start | bytes 3076
  (145 other events, 1424.2 us)
Sparse Core Ops, SparseCore 0:
  9.9 30.5 all-gather.29
  42.4 27.8 all-gather.25
  72.2 27.9 all-gather.27
  102.2 45.9 all-gather.47
  150.1 44.6 all-gather.39
  196.8 44.6 all-gather.45
  243.7 44.6 all-gather.37
  290.2 26.5 all-gather.31
  318.8 54.3 all-gather.33
  374.9 54.3 all-gather.35
  500.5 43.6 reduce-scatter.32
  546.5 43.2 reduce-scatter.34
  592.1 43.1 reduce-scatter.24
  637.6 43.1 reduce-scatter.26
  687.8 45.2 all-gather.43
  735.1 44.6 all-gather.41
  836.7 42.4 reduce-scatter.30
  881.5 43.1 reduce-scatter.28
  928.0 40.4 reduce-scatter.54
  972.0 41.2 reduce-scatter.58
  1016.6 41.1 reduce-scatter.56
  1061.5 41.2 reduce-scatter.40
  1106.0 41.1 reduce-scatter.36
  1150.7 41.2 reduce-scatter.38
  1195.3 41.1 reduce-scatter.48
  1240.0 41.2 reduce-scatter.52
  1284.4 41.1 reduce-scatter.50
  1329.3 41.2 reduce-scatter.46
  1373.8 41.1 reduce-scatter.42
  1418.5 41.2 reduce-scatter.44
  1463.3 71.2 reduce-scatter.64
  1538.4 71.2 reduce-scatter.60
  1613.1 71.2 reduce-scatter.62
  1688.2 71.2 reduce-scatter.70
  1763.0 71.2 reduce-scatter.66
  1838.0 71.2 reduce-scatter.68
  1913.2 123.3 all-reduce.25
where the time goes:
time: 2060 us
  waiting for transfers between devices  1320 us (64%)
  matrix products  479 us (23%)
  blocking collectives  99.5 us (5%)
  other arithmetic  98.5 us (5%)
  local copies, waits for them, and re-layouts  42 us (2%)
    reduce_scatter x3, waiting for transfers between devices, per_device(): lax.psum_scatter(local_grads[9].astype(jnp.bfloat16), 'fsdp', scatter_dim...  223 us
    reduce_scatter x3, waiting for transfers between devices, per_device(): lax.psum_scatter(local_grads[11].astype(jnp.bfloat16), 'fsdp', scatter_di...  222 us
    reduce_scatter x3, waiting for transfers between devices, per_device(): lax.psum_scatter(local_grads[3].astype(jnp.bfloat16), 'fsdp', scatter_dim...  132 us
    reduce_scatter x3, waiting for transfers between devices, per_device(): lax.psum_scatter(local_grads[2].astype(jnp.bfloat16), 'fsdp', scatter_dim...  132 us
    reduce_scatter x3, waiting for transfers between devices, per_device(): lax.psum_scatter(local_grads[4].astype(jnp.bfloat16), 'fsdp', scatter_dim...  128 us
    all_gather x3, waiting for transfers between devices, per_device(): lax.all_gather(values_local.reshape(num_rows, local_len, model_width), 's...  100 us
    dot_general x18, matrix products, back_dot(): lax.dot_general(left, right, (((1,), (1,)), ((), ())), preferred_element_...  84.1 us
    dot_general x18, matrix products, token_dot(): lax.dot_general(left, right, (((0,), (0,)), ((), ())), preferred_element_...  78.6 us
  transfers between devices with their start and end apart: 37, of which 32 were waited for; matrix products, arithmetic and copies ran while one was open for 22% of the time, Pallas kernels for 0%

commit v1 on v0

--- a/solution.py
+++ b/solution.py
@@ -6,6 +6,10 @@
 epsilon = 1e-05
 masked_out = -1e30
 EXACT_PRECISION = lax.Precision.HIGHEST
+
+
+def _serve_ports(x_part, chip_axis):
+    return lax.all_gather(x_part, axis_name=chip_axis).sum(axis=0)
 
 
 def layer_norm(field, norm_gain, norm_shift):
@@ -317,7 +321,7 @@
     totals = (
         lax.psum(summed[0].astype(jnp.bfloat16), "seq").astype(jnp.float32),
         lax.psum(summed[1].astype(jnp.bfloat16), "seq").astype(jnp.float32),
-        lax.psum(summed[2].astype(jnp.bfloat16), "seq").astype(jnp.float32),
+        _serve_ports(summed[2].astype(jnp.bfloat16), "seq").astype(jnp.float32),
         lax.psum(summed[3].astype(jnp.bfloat16), "seq").astype(jnp.float32),
         lax.psum(summed[4].astype(jnp.bfloat16), "seq").astype(jnp.float32),
         lax.psum(summed[5].astype(jnp.bfloat16), "seq").astype(jnp.float32),

time: 2060 us -> 2080 us (level)
    reduce_scatter x3, waiting for transfers between devices: 24.4 us -> 132 us  [per_device(): lax.psum_scatter(local_grads[5].astype(jnp.bfloat16), 'fsdp', scatter_dim...]
    reduce_scatter x3, waiting for transfers between devices: 132 us -> 24.9 us  [per_device(): lax.psum_scatter(local_grads[2].astype(jnp.bfloat16), 'fsdp', scatter_dim...]
  transfers between devices with their start and end apart: 37 -> 38, of which waited for: 32 -> 32; matrix products, arithmetic and copies ran while one was open for 22% -> 22% of each run, Pallas kernels for 0% -> 0%
where the time goes in v1:
time: 2080 us
  waiting for transfers between devices  1340 us (64%)
  matrix products  480 us (23%)
  blocking collectives  99 us (5%)
  other arithmetic  98.9 us (5%)
  local copies, waits for them, and re-layouts  41.6 us (2%)
    reduce_scatter x3, waiting for transfers between devices, per_device(): lax.psum_scatter(local_grads[11].astype(jnp.bfloat16), 'fsdp', scatter_di...  223 us
    reduce_scatter x3, waiting for transfers between devices, per_device(): lax.psum_scatter(local_grads[9].astype(jnp.bfloat16), 'fsdp', scatter_dim...  221 us
    reduce_scatter x3, waiting for transfers between devices, per_device(): lax.psum_scatter(local_grads[3].astype(jnp.bfloat16), 'fsdp', scatter_dim...  132 us
    reduce_scatter x3, waiting for transfers between devices, per_device(): lax.psum_scatter(local_grads[5].astype(jnp.bfloat16), 'fsdp', scatter_dim...  132 us
    reduce_scatter x3, waiting for transfers between devices, per_device(): lax.psum_scatter(local_grads[4].astype(jnp.bfloat16), 'fsdp', scatter_dim...  128 us
    all_gather x3, waiting for transfers between devices, per_device(): lax.all_gather(values_local.reshape(num_rows, local_len, model_width), 's...  100 us
    psum x1, waiting for transfers between devices, per_device(): lax.psum(summed[3].astype(jnp.bfloat16), 'seq').astype(jnp.float32)  89.2 us
    dot_general x18, matrix products, back_dot(): lax.dot_general(left, right, (((1,), (1,)), ((), ())), preferred_element_...  88.8 us
  transfers between devices with their start and end apart: 38, of which 32 were waited for; matrix products, arithmetic and copies ran while one was open for 22% of the time, Pallas kernels for 0%

profile of v1, /device:TPU:0, one launch (start us, length us, event | category | flops | bytes accessed | tf_op | source)
XLA Modules:
  0.0 2077.6 jit_solution(7250930133436004529)
XLA Ops:
  9.5 10.3 all-gather.7
  19.8 8.6 all-gather.8
  32.4 8.1 all-gather.32.cloned.1.call-done
  47.2 23.2 %all-gather.28.cloned.1.call-done = bf16[1024,1024]{1,0:T(8,128)(2,1)} async-done(((bf16[128,1024]{1,0:T(8,128)(2,1)}), bf16[1024,1024]{1,0:T(8,128)(2,1)}) %all-gather.28.cloned.1.call-update) | async-done | bytes 2097168 | tf_op jit(solution)/shard_map/all_gather | solution.py:86
  79.1 8.7 all-gather.10
  87.8 7.8 all-gather.11
  95.6 8.8 all-gather.9
  104.5 8.2 all-gather.12
  116.1 9.2 fusion.3
  132.6 15.5 all-gather.50.cloned.1.call-done
  151.0 22.1 %fusion.231 = (f32[16,256]{1,0:T(8,128)S(1)}, f32[16,256,1024]{2,1,0:T(8,128)}) fusion(f32[256,1024,16]{1,2,0:T(8,128)} %fusion.3, bf16[256,16,64]{0,2,1:T(8,128)(2,1)S(1)} %bitcast.440, bf16[1024,16,64]{0,2,1:T(8,128)(2,1)S(1)} %bitcast.429, pred[256,1024]{1,0:T(8,128)(4,1)S(1)} %get-tuple-element.106), kind=kOutput, calls=%fused_computation.386 | convolution fusion | flops 553644032 | bytes 36454400 | tf_op jit(solution)/shard_map/rqhd,rkhd->rhqk/dot_general | solution.py:146
  180.9 14.0 all-gather.42.cloned.1.call-done
  197.7 43.8 %all-gather.48.cloned.1.call-done = bf16[1024,1024]{1,0:T(8,128)(2,1)} async-done(((bf16[256,1024]{1,0:T(8,128)(2,1)}), bf16[1024,1024]{1,0:T(8,128)(2,1)}) %all-gather.48.cloned.1.call-update) | async-done | bytes 2097168 | tf_op jit(solution)/shard_map/all_gather | solution.py:133
  245.5 42.9 %all-gather.40.cloned.1.call-done = bf16[1024,1024]{1,0:T(8,128)(2,1)} async-done(((bf16[256,1024]{1,0:T(8,128)(2,1)}), bf16[1024,1024]{1,0:T(8,128)(2,1)}) %all-gather.40.cloned.1.call-update) | async-done | bytes 2097168 | tf_op jit(solution)/shard_map/all_gather | solution.py:133
  292.3 9.2 fusion.83
  301.5 15.4 all-gather.34.cloned.1.call-done
  319.9 21.5 %fusion.233 = (f32[16,256]{1,0:T(8,128)S(1)}, f32[16,256,1024]{2,1,0:T(8,128)}) fusion(f32[256,1024,16]{1,2,0:T(8,128)} %fusion.3, bf16[256,16,64]{0,2,1:T(8,128)(2,1)S(1)} %bitcast.438, bf16[1024,16,64]{0,2,1:T(8,128)(2,1)S(1)} %bitcast.431, pred[256,1024]{1,0:T(8,128)(4,1)S(1)} %get-tuple-element.107), kind=kOutput, calls=%fused_computation.388 | convolution fusion | flops 553644032 | bytes 36454400 | tf_op jit(solution)/shard_map/rqhd,rkhd->rhqk/dot_general | solution.py:146
  341.4 9.2 fusion.11
  362.6 10.6 all-gather.36.cloned.1.call-done
  373.2 16.4 multiply_convert_fusion.6
  389.6 16.4 multiply_convert_fusion.8
  406.1 23.3 %all-gather.38.cloned.1.call-done = bf16[4096,1024]{1,0:T(8,128)(2,1)} async-done(((bf16[512,1024]{1,0:T(8,128)(2,1)}), bf16[4096,1024]{1,0:T(8,128)(2,1)}) %all-gather.38.cloned.1.call-update) | async-done | bytes 8388624 | tf_op jit(solution)/shard_map/all_gather | solution.py:93
  429.4 12.4 fusion.239
  448.6 11.7 fusion.237
  471.6 15.1 multiply_reduce_fusion
  488.6 7.9 multiply_convert_fusion
  500.5 9.1 fusion.56
  513.2 14.6 multiply_reduce_fusion.2
  530.4 7.8 multiply_convert_fusion.2
  542.3 9.2 fusion.50
  571.6 18.2 reduce-scatter.35.cloned.1.call-done
  593.6 41.7 %reduce-scatter.25.cloned.1.call-done = bf16[1,256,1024]{1,2,0:T(8,128)(2,1)} async-done(((bf16[1,1024,1024]{1,2,0:T(8,128)(2,1)}), bf16[1,256,1024]{1,2,0:T(8,128)(2,1)}) %reduce-scatter.25.cloned.1.call-update) | async-done | bytes 524304 | tf_op jit(solution)/shard_map/reduce_scatter | solution.py:234
  638.8 42.0 %reduce-scatter.27.cloned.1.call-done = bf16[1,256,1024]{1,2,0:T(8,128)(2,1)} async-done(((bf16[1,1024,1024]{1,2,0:T(8,128)(2,1)}), bf16[1,256,1024]{1,2,0:T(8,128)(2,1)}) %reduce-scatter.27.cloned.1.call-update) | async-done | bytes 524304 | tf_op jit(solution)/shard_map/reduce_scatter | solution.py:240
  693.5 39.6 %all-gather.46.cloned.1.call-done = bf16[1024,1024]{1,0:T(8,128)(2,1)} async-done(((bf16[256,1024]{1,0:T(8,128)(2,1)}), bf16[1024,1024]{1,0:T(8,128)(2,1)}) %all-gather.46.cloned.1.call-update) | async-done | bytes 2097168 | tf_op jit(solution)/shard_map/all_gather | solution.py:130
  736.4 22.2 %fusion.235 = (f32[16,256]{1,0:T(8,128)S(1)}, f32[16,256,1024]{2,1,0:T(8,128)}) fusion(f32[256,1024,16]{1,2,0:T(8,128)} %fusion.3, bf16[256,16,64]{0,2,1:T(8,128)(2,1)S(1)} %bitcast.442, bf16[1024,16,64]{0,2,1:T(8,128)(2,1)S(1)} %bitcast.433, pred[256,1024]{1,0:T(8,128)(4,1)S(1)} %copy-done.46), kind=kOutput, calls=%fused_computation.390 | convolution fusion | flops 553644032 | bytes 36454400 | tf_op jit(solution)/shard_map/rqhd,rkhd->rhqk/dot_general | solution.py:146
  766.3 13.5 all-gather.44.cloned.1.call-done
  782.6 8.3 fusion.84
  793.4 15.7 multiply_convert_fusion.7
  809.1 11.6 fusion.238
  831.3 9.2 fusion.53
  840.6 9.9 multiply_reduce_fusion.1
  850.4 7.8 multiply_convert_fusion.1
  898.7 30.0 %reduce-scatter.29.cloned.1.call-done = bf16[1,256,1024]{1,2,0:T(8,128)(2,1)} async-done(((bf16[1,1024,1024]{1,2,0:T(8,128)(2,1)}), bf16[1,256,1024]{1,2,0:T(8,128)(2,1)}) %reduce-scatter.29.cloned.1.call-update) | async-done | bytes 524304 | tf_op jit(solution)/shard_map/reduce_scatter | solution.py:234
  971.9 7.8 convolution_convert_fusion.4
  982.9 8.9 all-gather.13
  1037.0 24.9 %reduce-scatter.39.cloned.1.call-done = bf16[128,1024]{1,0:T(8,128)(2,1)} async-done(((bf16[1024,1024]{1,0:T(8,128)(2,1)}), bf16[128,1024]{1,0:T(8,128)(2,1)}) %reduce-scatter.39.cloned.1.call-update) | async-done | bytes 262160 | tf_op jit(solution)/shard_map/reduce_scatter | solution.py:286
  1064.2 42.6 %reduce-scatter.55.cloned.1.call-done = bf16[128,1024]{1,0:T(8,128)(2,1)} async-done(((bf16[1024,1024]{1,0:T(8,128)(2,1)}), bf16[128,1024]{1,0:T(8,128)(2,1)}) %reduce-scatter.55.cloned.1.call-update) | async-done | bytes 262160 | tf_op jit(solution)/shard_map/reduce_scatter | solution.py:295
  1106.8 44.5 %reduce-scatter.59.cloned.1.call-done = bf16[128,1024]{1,0:T(8,128)(2,1)} async-done(((bf16[1024,1024]{1,0:T(8,128)(2,1)}), bf16[128,1024]{1,0:T(8,128)(2,1)}) %reduce-scatter.59.cloned.1.call-update) | async-done | bytes 262160 | tf_op jit(solution)/shard_map/reduce_scatter | solution.py:295
  1151.4 44.7 %reduce-scatter.57.cloned.1.call-done = bf16[128,1024]{1,0:T(8,128)(2,1)} async-done(((bf16[1024,1024]{1,0:T(8,128)(2,1)}), bf16[128,1024]{1,0:T(8,128)(2,1)}) %reduce-scatter.57.cloned.1.call-update) | async-done | bytes 262160 | tf_op jit(solution)/shard_map/reduce_scatter | solution.py:295
  1201.8 38.9 %reduce-scatter.49.cloned.1.call-done = bf16[128,1024]{1,0:T(8,128)(2,1)} async-done(((bf16[1024,1024]{1,0:T(8,128)(2,1)}), bf16[128,1024]{1,0:T(8,128)(2,1)}) %reduce-scatter.49.cloned.1.call-update) | async-done | bytes 262160 | tf_op jit(solution)/shard_map/reduce_scatter | solution.py:292
  1240.6 44.7 %reduce-scatter.53.cloned.1.call-done = bf16[128,1024]{1,0:T(8,128)(2,1)} async-done(((bf16[1024,1024]{1,0:T(8,128)(2,1)}), bf16[128,1024]{1,0:T(8,128)(2,1)}) %reduce-scatter.53.cloned.1.call-update) | async-done | bytes 262160 | tf_op jit(solution)/shard_map/reduce_scatter | solution.py:292
  1285.4 44.4 %reduce-scatter.51.cloned.1.call-done = bf16[128,1024]{1,0:T(8,128)(2,1)} async-done(((bf16[1024,1024]{1,0:T(8,128)(2,1)}), bf16[128,1024]{1,0:T(8,128)(2,1)}) %reduce-scatter.51.cloned.1.call-update) | async-done | bytes 262160 | tf_op jit(solution)/shard_map/reduce_scatter | solution.py:292
  1331.7 42.9 %reduce-scatter.47.cloned.1.call-done = bf16[128,1024]{1,0:T(8,128)(2,1)} async-done(((bf16[1024,1024]{1,0:T(8,128)(2,1)}), bf16[128,1024]{1,0:T(8,128)(2,1)}) %reduce-scatter.47.cloned.1.call-update) | async-done | bytes 262160 | tf_op jit(solution)/shard_map/reduce_scatter | solution.py:289
  1374.6 44.5 %reduce-scatter.43.cloned.1.call-done = bf16[128,1024]{1,0:T(8,128)(2,1)} async-done(((bf16[1024,1024]{1,0:T(8,128)(2,1)}), bf16[128,1024]{1,0:T(8,128)(2,1)}) %reduce-scatter.43.cloned.1.call-update) | async-done | bytes 262160 | tf_op jit(solution)/shard_map/reduce_scatter | solution.py:289
  1419.2 44.7 %reduce-scatter.45.cloned.1.call-done = bf16[128,1024]{1,0:T(8,128)(2,1)} async-done(((bf16[1024,1024]{1,0:T(8,128)(2,1)}), bf16[128,1024]{1,0:T(8,128)(2,1)}) %reduce-scatter.45.cloned.1.call-update) | async-done | bytes 262160 | tf_op jit(solution)/shard_map/reduce_scatter | solution.py:289
  1465.8 72.8 %reduce-scatter.71.cloned.1.call-done = bf16[512,1024]{1,0:T(8,128)(2,1)} async-done(((bf16[4096,1024]{1,0:T(8,128)(2,1)}), bf16[512,1024]{1,0:T(8,128)(2,1)}) %reduce-scatter.71.cloned.1.call-update) | async-done | bytes 1048592 | tf_op jit(solution)/shard_map/reduce_scatter | solution.py:313
  1538.7 75.2 %reduce-scatter.67.cloned.1.call-done = bf16[512,1024]{1,0:T(8,128)(2,1)} async-done(((bf16[4096,1024]{1,0:T(8,128)(2,1)}), bf16[512,1024]{1,0:T(8,128)(2,1)}) %reduce-scatter.67.cloned.1.call-update) | async-done | bytes 1048592 | tf_op jit(solution)/shard_map/reduce_scatter | solution.py:313
  1613.8 74.6 %reduce-scatter.69.cloned.1.call-done = bf16[512,1024]{1,0:T(8,128)(2,1)} async-done(((bf16[4096,1024]{1,0:T(8,128)(2,1)}), bf16[512,1024]{1,0:T(8,128)(2,1)}) %reduce-scatter.69.cloned.1.call-update) | async-done | bytes 1048592 | tf_op jit(solution)/shard_map/reduce_scatter | solution.py:313
  1691.9 71.7 %reduce-scatter.65.cloned.1.call-done = bf16[128,4096]{1,0:T(8,128)(2,1)} async-done(((bf16[1024,4096]{1,0:T(8,128)(2,1)}), bf16[128,4096]{1,0:T(8,128)(2,1)}) %reduce-scatter.65.cloned.1.call-update) | async-done | bytes 1048592 | tf_op jit(solution)/shard_map/reduce_scatter | solution.py:307
  1763.6 74.8 %reduce-scatter.61.cloned.1.call-done = bf16[128,4096]{1,0:T(8,128)(2,1)} async-done(((bf16[1024,4096]{1,0:T(8,128)(2,1)}), bf16[128,4096]{1,0:T(8,128)(2,1)}) %reduce-scatter.61.cloned.1.call-update) | async-done | bytes 1048592 | tf_op jit(solution)/shard_map/reduce_scatter | solution.py:307
  1838.3 75.0 %reduce-scatter.63.cloned.1.call-done = bf16[128,4096]{1,0:T(8,128)(2,1)} async-done(((bf16[1024,4096]{1,0:T(8,128)(2,1)}), bf16[128,4096]{1,0:T(8,128)(2,1)}) %reduce-scatter.63.cloned.1.call-update) | async-done | bytes 1048592 | tf_op jit(solution)/shard_map/reduce_scatter | solution.py:307
  1923.3 25.3 %all-reduce.21 = (bf16[1024]{0:T(1024)(128)(2,1)S(1)}, bf16[1024]{0:T(1024)(128)(2,1)S(1)}, bf16[1024]{0:T(1024)(128)(2,1)S(1)}, bf16[1024]{0:T(1024)(128)(2,1)S...) all-reduce(bf16[1024]{0:T(1024)(128)(2,1)S(1)} %get-tuple-element.1, ...), channel_id=17, replica_groups=mesh['fsdp'=8,'seq'=4] {'fsdp'}, use_global_device_ids=true, to_apply=%region_46.47.clone | all-reduce | flops 29184 | bytes 116736
  1949.2 12.4 all-reduce.22
  1971.7 89.2 %all-reduce.26.cloned.1.call-done = (bf16[128,1024]{1,0:T(8,128)(2,1)}, bf16[128,1024]{1,0:T(8,128)(2,1)}, bf16[128,1024]{1,0:T(8,128)(2,1)}, bf16[128,4096]{1,0:T(8,128)(2,1)}, bf16[512,1024]{1,0:T(8,128)(2,1)}) async-done(((bf16[128,1024]{1,0:T(8,128)(2,1)}, bf16[128,1024]{1,0:T(8,128)(2,1)}, bf16[128,1024]{1,0:T(8,128)(2,1)}, bf16[128,4096]{1,0:T(8,128)(2,1)}, bf16[512,1024]{1,0:T(8,128)(2,1)}), ...) | async-done | bytes 2883600 | tf_op jit(solution)/shard_map/psum | solution.py:325
  (570 shorter events, 343.6 us)
Async XLA Ops:
  7.2 33.4 %all-gather.32.cloned.1.call-start = ((), (), s32[]{:S(2)}) async-start(), calls=%async_computation.26 | async-start | bytes 2359296 | tf_op jit(solution)/shard_map/all_gather | solution.py:85
  7.9 62.4 %all-gather.28.cloned.1.call-start = ((), (), s32[]{:S(2)}) async-start(), calls=%async_computation.24 | async-start | bytes 2359296 | tf_op jit(solution)/shard_map/all_gather | solution.py:86
  8.7 118.0 %all-gather.30.cloned.1.call-start = ((), (), s32[]{:S(2)}) async-start(), calls=%async_computation.25 | async-start | bytes 2359296 | tf_op jit(solution)/shard_map/all_gather | solution.py:84
  9.4 138.7 %all-gather.50.cloned.1.call-start = ((), (), s32[]{:S(2)}) async-start(), calls=%async_computation.59 | async-start | bytes 2621440 | tf_op jit(solution)/shard_map/all_gather | solution.py:130
  19.8 110.2 %copy-start.81 = (f32[8,1,128]{2,1,0:T(1,128)}, f32[8,1,128]{2,1,0:T(1,128)S(1)}, u32[]{:S(2)}) copy-start(f32[8,1,128]{2,1,0:T(1,128)S(1)} %convert_element_type.940) | copy-start | bytes 12292
  28.4 101.6 %copy-start.128 = (f32[8,1,128]{2,1,0:T(1,128)}, f32[8,1,128]{2,1,0:T(1,128)S(1)}, u32[]{:S(2)}) copy-start(f32[8,1,128]{2,1,0:T(1,128)S(1)} %convert_element_type.941) | copy-start | bytes 12292
  30.6 96.0 %copy-start.104 = (f32[256]{0:T(256)}, f32[256]{0:T(256)S(1)}, u32[]{:S(2)}) copy-start(f32[256]{0:T(256)S(1)} %get-tuple-element.140) | copy-start | bytes 3076
  30.6 99.4 %copy-start.107 = (f32[256]{0:T(256)}, f32[256]{0:T(256)S(1)}, u32[]{:S(2)}) copy-start(f32[256]{0:T(256)S(1)} %get-tuple-element.139) | copy-start | bytes 3076
  32.4 97.6 %copy-start.123 = (f32[256]{0:T(256)}, f32[256]{0:T(256)S(1)}, u32[]{:S(2)}) copy-start(f32[256]{0:T(256)S(1)} %fusion.186) | copy-start | bytes 3076
  43.9 151.0 %all-gather.42.cloned.1.call-start = ((), (), s32[]{:S(2)}) async-start(), calls=%async_computation.55 | async-start | bytes 2621440 | tf_op jit(solution)/shard_map/all_gather | solution.py:130
  44.0 82.7 %copy-start.121 = (f32[256]{0:T(256)}, f32[256]{0:T(256)S(1)}, u32[]{:S(2)}) copy-start(f32[256]{0:T(256)S(1)} %fusion.182) | copy-start | bytes 3076
  47.1 194.4 %all-gather.48.cloned.1.call-start = ((), (), s32[]{:S(2)}) async-start(), calls=%async_computation.58 | async-start | bytes 2621440 | tf_op jit(solution)/shard_map/all_gather | solution.py:133
  73.6 214.8 %all-gather.40.cloned.1.call-start = ((), (), s32[]{:S(2)}) async-start(), calls=%async_computation.54 | async-start | bytes 2621440 | tf_op jit(solution)/shard_map/all_gather | solution.py:133
  76.8 240.1 %all-gather.34.cloned.1.call-start = ((), (), s32[]{:S(2)}) async-start(), calls=%async_computation.27 | async-start | bytes 2359296 | tf_op jit(solution)/shard_map/all_gather | solution.py:87
  77.5 295.7 %all-gather.36.cloned.1.call-start = ((), (), s32[]{:S(2)}) async-start(), calls=%async_computation.28 | async-start | bytes 9437184 | tf_op jit(solution)/shard_map/all_gather | solution.py:91
  78.3 351.1 %all-gather.38.cloned.1.call-start = ((), (), s32[]{:S(2)}) async-start(), calls=%async_computation.29 | async-start | bytes 9437184 | tf_op jit(solution)/shard_map/all_gather | solution.py:93
  78.8 489.4 %reduce-scatter.33.cloned.1.call-start = ((), (), s32[]{:S(2)}) async-start(), calls=%async_computation.34 | async-start | bytes 2621440 | tf_op jit(solution)/shard_map/reduce_scatter | solution.py:234
  95.6 293.9 %copy-start.69 = (f32[8,1,128]{2,1,0:T(1,128)}, f32[8,1,128]{2,1,0:T(1,128)S(1)}, u32[]{:S(2)}) copy-start(f32[8,1,128]{2,1,0:T(1,128)S(1)} %convert_element_type.943) | copy-start | bytes 12292
  112.7 276.9 %copy-start.91 = (f32[8,1,512]{2,1,0:T(1,128)}, f32[8,1,512]{2,1,0:T(1,128)S(1)}, u32[]{:S(2)}) copy-start(f32[8,1,512]{2,1,0:T(1,128)S(1)} %convert_element_type.944) | copy-start | bytes 49156
  132.6 40.5 %copy-start.33 = (bf16[256,1024]{0,1:T(8,128)(2,1)}, bf16[256,1024]{0,1:T(8,128)(2,1)S(1)}, u32[]{:S(2)}) copy-start(bf16[256,1024]{0,1:T(8,128)(2,1)S(1)} %copy.104) | copy-start | bytes 1572868
  197.7 122.2 %copy-start.6 = (bf16[1024,1024]{0,1:T(8,128)(2,1)}, bf16[1024,1024]{0,1:T(8,128)(2,1)S(1)}, u32[]{:S(2)}) copy-start(bf16[1024,1024]{0,1:T(8,128)(2,1)S(1)} %copy.97) | copy-start | bytes 6291460
  319.6 148.4 %copy-start.18 = (f32[256,1024]{1,0:T(8,128)}, f32[256,1024]{1,0:T(8,128)S(1)}, u32[]{:S(2)}) copy-start(f32[256,1024]{1,0:T(8,128)S(1)} %get-tuple-element.111) | copy-start | bytes 3145732
  319.6 148.4 %copy-start.85 = (f32[256]{0:T(256)}, f32[256]{0:T(256)S(1)}, u32[]{:S(2)}) copy-start(f32[256]{0:T(256)S(1)} %broadcast_multiply_fusion) | copy-start | bytes 3076
  360.8 107.3 %copy-start.87 = (f32[256]{0:T(256)}, f32[256]{0:T(256)S(1)}, u32[]{:S(2)}) copy-start(f32[256]{0:T(256)S(1)} %broadcast_multiply_fusion.4) | copy-start | bytes 3076
  362.0 106.0 %copy-start.95 = (f32[256]{0:T(256)}, f32[256]{0:T(256)S(1)}, u32[]{:S(2)}) copy-start(f32[256]{0:T(256)S(1)} %fusion.187) | copy-start | bytes 3076
  362.0 106.0 %copy-start.93 = (f32[256]{0:T(256)}, f32[256]{0:T(256)S(1)}, u32[]{:S(2)}) copy-start(f32[256]{0:T(256)S(1)} %fusion.183) | copy-start | bytes 3076
  469.8 40.5 %copy-start.60 = (bf16[256,1024]{1,0:T(8,128)(2,1)}, bf16[256,1024]{1,0:T(8,128)(2,1)S(1)}, u32[]{:S(2)}) copy-start(bf16[256,1024]{1,0:T(8,128)(2,1)S(1)} %get-tuple-element.96) | copy-start | bytes 1572868
  500.4 89.4 %reduce-scatter.35.cloned.1.call-start = ((), (), s32[]{:S(2)}) async-start(), calls=%async_computation.35 | async-start | bytes 2621440 | tf_op jit(solution)/shard_map/reduce_scatter | solution.py:240
  509.6 125.7 %reduce-scatter.25.cloned.1.call-start = ((), (), s32[]{:S(2)}) async-start(), calls=%async_computation.30 | async-start | bytes 2621440 | tf_op jit(solution)/shard_map/reduce_scatter | solution.py:234
  542.2 138.5 %reduce-scatter.27.cloned.1.call-start = ((), (), s32[]{:S(2)}) async-start(), calls=%async_computation.31 | async-start | bytes 2621440 | tf_op jit(solution)/shard_map/reduce_scatter | solution.py:240
  551.5 181.6 %all-gather.46.cloned.1.call-start = ((), (), s32[]{:S(2)}) async-start(), calls=%async_computation.57 | async-start | bytes 2621440 | tf_op jit(solution)/shard_map/all_gather | solution.py:130
  551.8 139.1 %copy-start.98 = (f32[256]{0:T(256)}, f32[256]{0:T(256)S(1)}, u32[]{:S(2)}) copy-start(f32[256]{0:T(256)S(1)} %broadcast_multiply_fusion.3) | copy-start | bytes 3076
  571.6 109.1 %copy-start.11 = (bf16[3,1,256,1024]{3,2,1,0:T(8,128)(2,1)S(1)}, bf16[3,1,256,1024]{3,2,1,0:T(8,128)(2,1)}, u32[]{:S(2)}) copy-start(bf16[3,1,256,1024]{3,2,1,0:T(8,128)(2,1)} %param.17) | copy-start | bytes 4718596
  571.6 109.1 %copy-start.82 = (f32[8,1,128]{2,1,0:T(1,128)S(1)}, f32[8,1,128]{2,1,0:T(1,128)}, u32[]{:S(2)}) copy-start(f32[8,1,128]{2,1,0:T(1,128)} %copy-done.81) | copy-start | bytes 12292
  571.6 109.1 %copy-start.105 = (f32[256]{0:T(256)S(1)}, f32[256]{0:T(256)}, u32[]{:S(2)}) copy-start(f32[256]{0:T(256)} %copy-done.104) | copy-start | bytes 3076
  571.6 109.1 %copy-start.108 = (f32[256]{0:T(256)S(1)}, f32[256]{0:T(256)}, u32[]{:S(2)}) copy-start(f32[256]{0:T(256)} %copy-done.107) | copy-start | bytes 3076
  638.8 47.2 %copy-start.129 = (f32[8,1,128]{2,1,0:T(1,128)S(1)}, f32[8,1,128]{2,1,0:T(1,128)}, u32[]{:S(2)}) copy-start(f32[8,1,128]{2,1,0:T(1,128)} %copy-done.128) | copy-start | bytes 12292
  687.6 92.1 %all-gather.44.cloned.1.call-start = ((), (), s32[]{:S(2)}) async-start(), calls=%async_computation.56 | async-start | bytes 2621440 | tf_op jit(solution)/shard_map/all_gather | solution.py:133
  690.9 45.5 %copy-start.46 = (pred[256,1024]{1,0:T(8,128)(4,1)S(1)}, pred[256,1024]{1,0:T(8,128)(4,1)}, u32[]{:S(2)}) copy-start(pred[256,1024]{1,0:T(8,128)(4,1)} %get-tuple-element.105) | copy-start | bytes 786436
  690.9 199.9 %reduce-scatter.31.cloned.1.call-start = ((), (), s32[]{:S(2)}) async-start(), calls=%async_computation.33 | async-start | bytes 2621440 | tf_op jit(solution)/shard_map/reduce_scatter | solution.py:240
  766.3 65.0 %copy-start.75 = (f32[16,256]{1,0:T(8,128)}, f32[16,256]{1,0:T(8,128)S(1)}, u32[]{:S(2)}) copy-start(f32[16,256]{1,0:T(8,128)S(1)} %log_add_fusion.1) | copy-start | bytes 49156
  840.5 88.2 %reduce-scatter.29.cloned.1.call-start = ((), (), s32[]{:S(2)}) async-start(), calls=%async_computation.32 | async-start | bytes 2621440 | tf_op jit(solution)/shard_map/reduce_scatter | solution.py:234
  862.2 174.8 %reduce-scatter.41.cloned.1.call-start = ((), (), s32[]{:S(2)}) async-start(), calls=%async_computation.38 | async-start | bytes 2359296 | tf_op jit(solution)/shard_map/reduce_scatter | solution.py:286
  865.6 171.4 %reduce-scatter.37.cloned.1.call-start = ((), (), s32[]{:S(2)}) async-start(), calls=%async_computation.36 | async-start | bytes 2359296 | tf_op jit(solution)/shard_map/reduce_scatter | solution.py:286
  869.1 192.8 %reduce-scatter.39.cloned.1.call-start = ((), (), s32[]{:S(2)}) async-start(), calls=%async_computation.37 | async-start | bytes 2359296 | tf_op jit(solution)/shard_map/reduce_scatter | solution.py:286
  879.3 227.5 %reduce-scatter.55.cloned.1.call-start = ((), (), s32[]{:S(2)}) async-start(), calls=%async_computation.45 | async-start | bytes 2359296 | tf_op jit(solution)/shard_map/reduce_scatter | solution.py:295
  881.4 269.9 %reduce-scatter.59.cloned.1.call-start = ((), (), s32[]{:S(2)}) async-start(), calls=%async_computation.47 | async-start | bytes 2359296 | tf_op jit(solution)/shard_map/reduce_scatter | solution.py:295
  883.6 312.6 %reduce-scatter.57.cloned.1.call-start = ((), (), s32[]{:S(2)}) async-start(), calls=%async_computation.46 | async-start | bytes 2359296 | tf_op jit(solution)/shard_map/reduce_scatter | solution.py:295
  886.1 354.5 %reduce-scatter.49.cloned.1.call-start = ((), (), s32[]{:S(2)}) async-start(), calls=%async_computation.42 | async-start | bytes 2359296 | tf_op jit(solution)/shard_map/reduce_scatter | solution.py:292
  888.4 397.0 %reduce-scatter.53.cloned.1.call-start = ((), (), s32[]{:S(2)}) async-start(), calls=%async_computation.44 | async-start | bytes 2359296 | tf_op jit(solution)/shard_map/reduce_scatter | solution.py:292
  890.7 439.0 %reduce-scatter.51.cloned.1.call-start = ((), (), s32[]{:S(2)}) async-start(), calls=%async_computation.43 | async-start | bytes 2359296 | tf_op jit(solution)/shard_map/reduce_scatter | solution.py:292
  894.1 480.5 %reduce-scatter.47.cloned.1.call-start = ((), (), s32[]{:S(2)}) async-start(), calls=%async_computation.41 | async-start | bytes 2359296 | tf_op jit(solution)/shard_map/reduce_scatter | solution.py:289
  896.4 522.8 %reduce-scatter.43.cloned.1.call-start = ((), (), s32[]{:S(2)}) async-start(), calls=%async_computation.39 | async-start | bytes 2359296 | tf_op jit(solution)/shard_map/reduce_scatter | solution.py:289
  898.7 565.2 %reduce-scatter.45.cloned.1.call-start = ((), (), s32[]{:S(2)}) async-start(), calls=%async_computation.40 | async-start | bytes 2359296 | tf_op jit(solution)/shard_map/reduce_scatter | solution.py:289
  932.0 606.7 %reduce-scatter.71.cloned.1.call-start = ((), (), s32[]{:S(2)}) async-start(), calls=%async_computation.53 | async-start | bytes 9437184 | tf_op jit(solution)/shard_map/reduce_scatter | solution.py:313
  939.4 674.4 %reduce-scatter.67.cloned.1.call-start = ((), (), s32[]{:S(2)}) async-start(), calls=%async_computation.51 | async-start | bytes 9437184 | tf_op jit(solution)/shard_map/reduce_scatter | solution.py:313
  946.9 741.5 %reduce-scatter.69.cloned.1.call-start = ((), (), s32[]{:S(2)}) async-start(), calls=%async_computation.52 | async-start | bytes 9437184 | tf_op jit(solution)/shard_map/reduce_scatter | solution.py:313
  954.4 809.2 %reduce-scatter.65.cloned.1.call-start = ((), (), s32[]{:S(2)}) async-start(), calls=%async_computation.50 | async-start | bytes 9437184 | tf_op jit(solution)/shard_map/reduce_scatter | solution.py:307
  962.8 875.5 %reduce-scatter.61.cloned.1.call-start = ((), (), s32[]{:S(2)}) async-start(), calls=%async_computation.48 | async-start | bytes 9437184 | tf_op jit(solution)/shard_map/reduce_scatter | solution.py:307
  971.2 942.1 %reduce-scatter.63.cloned.1.call-start = ((), (), s32[]{:S(2)}) async-start(), calls=%async_computation.49 | async-start | bytes 9437184 | tf_op jit(solution)/shard_map/reduce_scatter | solution.py:307
  979.7 989.7 %all-gather.52.cloned.1.call-start = ((), (), s32[]{:S(2)}) async-start(), calls=%async_computation.60 | async-start | bytes 1310720 | tf_op jit(solution)/shard_map/all_gather | solution.py:12
  1063.9 997.0 %all-reduce.26.cloned.1.call-start = ((), (), s32[]{:S(2)}) async-start(), calls=%async_computation.61 | async-start | bytes 5767168 | tf_op jit(solution)/shard_map/psum | solution.py:325
  1921.4 44.0 %copy-start.103 = (f32[256]{0:T(256)S(1)}, f32[256]{0:T(256)}, u32[]{:S(2)}) copy-start(f32[256]{0:T(256)} %copy-done.102) | copy-start | bytes 3076
  1921.4 44.0 %copy-start.115 = (f32[256]{0:T(256)S(1)}, f32[256]{0:T(256)}, u32[]{:S(2)}) copy-start(f32[256]{0:T(256)} %copy-done.114) | copy-start | bytes 3076
  (138 other events, 1127.5 us)
Sparse Core Ops, SparseCore 0:
  9.9 30.5 all-gather.31
  42.4 27.8 all-gather.27
  72.2 27.9 all-gather.29
  102.2 45.9 all-gather.49
  150.1 44.6 all-gather.41
  196.8 44.6 all-gather.47
  243.7 44.6 all-gather.39
  290.2 26.5 all-gather.33
  318.8 54.3 all-gather.35
  374.9 54.3 all-gather.37
  500.5 43.7 reduce-scatter.32
  546.6 43.1 reduce-scatter.34
  592.1 43.1 reduce-scatter.24
  637.6 43.1 reduce-scatter.26
  687.8 45.2 all-gather.45
  735.1 44.6 all-gather.43
  840.7 42.5 reduce-scatter.30
  885.5 43.1 reduce-scatter.28
  932.0 40.5 reduce-scatter.40
  976.1 41.3 reduce-scatter.36
  1020.8 41.1 reduce-scatter.38
  1065.6 41.2 reduce-scatter.54
  1110.1 41.1 reduce-scatter.58
  1154.9 41.2 reduce-scatter.56
  1199.4 41.1 reduce-scatter.48
  1244.1 41.2 reduce-scatter.52
  1288.5 41.1 reduce-scatter.50
  1333.4 41.2 reduce-scatter.46
  1377.9 41.1 reduce-scatter.42
  1422.7 41.2 reduce-scatter.44
  1467.4 71.2 reduce-scatter.70
  1542.5 71.2 reduce-scatter.66
  1617.1 71.2 reduce-scatter.68
  1692.3 71.2 reduce-scatter.64
  1767.0 71.2 reduce-scatter.60
  1842.0 71.2 reduce-scatter.62
  1915.3 27.9 all-gather.51
  1947.2 113.6 all-reduce.25
